TPU v7x, 32 devices: a whole 2x2x4 slice. The times are simulated.
32 devices in a mesh: row: 8 (over z, y), col: 4 (over x, core).
Axes of the slice: x: 2, y: 2, z: 4, core: 2. Of those that a mesh axis runs over, the one named last changes fastest.
Arguments:
- sequence: bfloat16 [128, 1024], P('row'), may hold values from -6 to 6
- pair_state: bfloat16 [128, 128, 128], P('row', 'col'), may hold values from -6 to 6
- residue_mask: int32 [128], replicated, may hold values 0 or 1
- chain_index: int32 [128], replicated, may hold values from 0 to 3, never falling along the last dimension, each value on 1 to 64 neighbouring positions
- attention_in: bfloat16 [1024, 4, 1024], P(None, None, 'col'), may hold values from -0.1875 to 0.1875
- attention_out: bfloat16 [1024, 1024], P('col'), may hold values from -0.1875 to 0.1875
- bias_weight: bfloat16 [128, 32], replicated, may hold values from -40 to 40
- chain_bias: float32 [32], replicated, may hold values from -2 to 2
- outer_in: bfloat16 [1024, 128], replicated, may hold values from -0.1875 to 0.1875
- outer_out: bfloat16 [128, 128], replicated, may hold values from -0.5 to 0.5
- triangle_in: bfloat16 [128, 5, 128], replicated, may hold values from -0.5 to 0.5
- triangle_out: bfloat16 [128, 128], replicated, may hold values from -0.5 to 0.5
- transition_up: bfloat16 [128, 512], replicated, may hold values from -0.5 to 0.5
- transition_down: bfloat16 [512, 128], replicated, may hold values from -0.25 to 0.25
Outputs:
- sequence_out: bfloat16 [128, 1024], P('row')
- pair_out: bfloat16 [128, 128, 128], P('row', 'col')
Inputs may be any that keep to these rules, and one draw needn't show every extreme that they name: chain_index never falls along the residues; each chain holds at most 64 residues.
All inputs are finite; a program needn't handle non-finite values.
Results may differ from a plain program's by a relative error of at most 0.0095.
The roundings to bfloat16 on the way count: a program that leaves them out, or rounds other values in their place, can miss the bound.
Values may be sent and summed in bfloat16 or wider, within the bound.
A program may use at most 64 MiB of HBM per device.

v0:
```python
import math
import jax
import jax.numpy as jnp
from jax import lax
from jax.sharding import PartitionSpec as P


def layer_norm(values):
    center = values - jnp.mean(values, axis=-1, keepdims=True)
    spread = jnp.mean(center * center, axis=-1, keepdims=True)
    return center * lax.rsqrt(spread + 1e-05)


def per_device(
    sequence,
    pair_state,
    residue_mask,
    chain_index,
    attention_in,
    attention_out,
    bias_weight,
    chain_bias,
    outer_in,
    outer_out,
    triangle_in,
    triangle_out,
    transition_up,
    transition_down,
):
    rows_here, cols_here, channels = pair_state.shape
    length_all = residue_mask.shape[0]
    row_index = lax.axis_index("row")
    col_index = lax.axis_index("col")
    row_start = row_index * rows_here
    col_start = col_index * cols_here
    pair_wide = pair_state.astype(jnp.float32)
    normed_pair = layer_norm(pair_wide).astype(jnp.bfloat16)
    bias_tile = jnp.einsum(
        "ijc,ch->hij", normed_pair, bias_weight, preferred_element_type=jnp.float32
    )
    pair_bias = lax.all_to_all(bias_tile, "col", split_axis=0, concat_axis=2, tiled=True)
    heads_here = pair_bias.shape[0]
    normed_seq = layer_norm(sequence.astype(jnp.float32)).astype(jnp.bfloat16)
    projected = jnp.einsum(
        "id,dpe->ipe", normed_seq, attention_in, preferred_element_type=jnp.float32
    )
    query = projected[:, 0].astype(jnp.bfloat16)
    key_rows = projected[:, 1].astype(jnp.bfloat16)
    value_rows = projected[:, 2].astype(jnp.bfloat16)
    gate = jax.nn.sigmoid(projected[:, 3])
    keys_all, values_all = (
        lax.all_gather(key_rows, "row", axis=0, tiled=True),
        lax.all_gather(value_rows, "row", axis=0, tiled=True),
    )
    head_width = query.shape[1] // heads_here
    query_heads = query.reshape(rows_here, heads_here, head_width)
    key_heads = keys_all.reshape(length_all, heads_here, head_width)
    value_heads = values_all.reshape(length_all, heads_here, head_width)
    scale = 1.0 / math.sqrt(head_width)
    scores = (
        jnp.einsum("ihd,jhd->hij", query_heads, key_heads, preferred_element_type=jnp.float32)
        * scale
    )
    chain_rows = lax.dynamic_slice_in_dim(chain_index, row_start, rows_here, 0)
    same_chain = (chain_rows[:, None] == chain_index[None, :]).astype(jnp.float32)
    head_offset = lax.dynamic_slice_in_dim(chain_bias, col_index * heads_here, heads_here, 0)
    scores = scores + pair_bias + head_offset[:, None, None] * same_chain[None]
    positions = jnp.arange(length_all, dtype=jnp.int32)
    query_ids = row_start + jnp.arange(rows_here, dtype=jnp.int32)
    allowed = (residue_mask[None, :] == 1) | (query_ids[:, None] == positions[None, :])
    allowed = allowed[None]
    highest = jnp.max(jnp.where(allowed, scores, -jnp.inf), axis=-1, keepdims=True)
    raised = jnp.where(allowed, jnp.exp(scores - highest), 0.0)
    weights = (raised / jnp.sum(raised, axis=-1, keepdims=True)).astype(jnp.bfloat16)
    gathered = jnp.einsum(
        "hij,jhd->ihd", weights, value_heads, preferred_element_type=jnp.float32
    ).reshape(rows_here, -1)
    mixed = (gate * gathered).astype(jnp.bfloat16)
    head_terms = jnp.dot(mixed, attention_out, preferred_element_type=jnp.float32)
    update = lax.psum(head_terms, "col")
    sequence_out = (sequence.astype(jnp.float32) + update).astype(jnp.bfloat16)
    normed_out = layer_norm(sequence_out.astype(jnp.float32)).astype(jnp.bfloat16)
    outer_rows = jnp.dot(normed_out, outer_in, preferred_element_type=jnp.float32).astype(
        jnp.bfloat16
    )
    half_width = outer_rows.shape[1] // 2
    right_all = lax.all_gather(outer_rows[:, half_width:], "row", axis=0, tiled=True)
    right_side = lax.dynamic_slice_in_dim(right_all, col_start, cols_here, 0).astype(jnp.float32)
    left_side = outer_rows[:, :half_width].astype(jnp.float32)
    outer_feat = jnp.concatenate(
        [
            left_side[:, None, :] * right_side[None, :, :],
            left_side[:, None, :] - right_side[None, :, :],
        ],
        axis=-1,
    ).astype(jnp.bfloat16)
    pair_mid = pair_wide + jnp.dot(
        outer_feat.reshape(-1, 2 * half_width), outer_out, preferred_element_type=jnp.float32
    ).reshape(rows_here, cols_here, channels)
    normed_mid = layer_norm(pair_mid).astype(jnp.bfloat16)
    tri = jnp.dot(
        normed_mid.reshape(-1, channels),
        triangle_in.reshape(channels, -1),
        preferred_element_type=jnp.float32,
    ).reshape(rows_here, cols_here, 5, channels)
    live = residue_mask.astype(jnp.float32)
    row_live = lax.dynamic_slice_in_dim(live, row_start, rows_here, 0)
    col_live = lax.dynamic_slice_in_dim(live, col_start, cols_here, 0)
    pair_live = (row_live[:, None] * col_live[None, :])[:, :, None]
    left_op = (jax.nn.sigmoid(tri[:, :, 0]) * tri[:, :, 1] * pair_live).astype(jnp.bfloat16)
    right_op = (jax.nn.sigmoid(tri[:, :, 2]) * tri[:, :, 3] * pair_live).astype(jnp.bfloat16)
    out_gate = jax.nn.sigmoid(tri[:, :, 4])
    column_all = lax.all_gather(right_op, "row", axis=0, tiled=True)
    crossed = lax.psum_scatter(
        jnp.einsum("jkc,ikc->jic", column_all, left_op, preferred_element_type=jnp.float32),
        "col",
        scatter_dimension=0,
        tiled=True,
    )
    product = jnp.transpose(crossed, (1, 0, 2))
    normed_product = layer_norm(product).astype(jnp.bfloat16)
    projected_product = jnp.dot(
        normed_product.reshape(-1, channels), triangle_out, preferred_element_type=jnp.float32
    ).reshape(rows_here, cols_here, channels)
    pair_late = pair_mid + out_gate * projected_product
    normed_late = layer_norm(pair_late).astype(jnp.bfloat16)
    hidden = jax.nn.relu(
        jnp.dot(
            normed_late.reshape(-1, channels), transition_up, preferred_element_type=jnp.float32
        )
    ).astype(jnp.bfloat16)
    lowered = jnp.dot(hidden, transition_down, preferred_element_type=jnp.float32).reshape(
        rows_here, cols_here, channels
    )
    pair_out = (pair_late + lowered).astype(jnp.bfloat16)
    return (sequence_out, pair_out)


def solution(mesh):
    return jax.shard_map(
        per_device,
        mesh=mesh,
        in_specs=(
            P("row", None),
            P("row", "col", None),
            P(),
            P(),
            P(None, None, "col"),
            P("col", None),
            P(),
            P(),
            P(),
            P(),
            P(),
            P(),
            P(),
            P(),
        ),
        out_specs=(P("row", None), P("row", "col", None)),
        check_vma=False,
    )
```

profile of v0, /device:TPU:0, one launch (start us, length us, event | category | flops | bytes accessed | tf_op | source)
XLA Modules:
  0.0 257.6 jit_solution(43655018280628967)
XLA Ops:
  7.2 1.2 convert_reduce_fusion
  8.4 1.2 fusion.14
  9.6 1.2 convolution_bitcast_fusion.1
  11.0 0.8 reshape.259
  11.8 4.2 %all-to-all-start = ((f32[4,1,4096]{2,1,0:T(1,128)}), f32[4,1,4096]{2,1,0:T(1,128)S(1)}, u32[]{:S(2)}, u32[]{:S(2)}) async-start(f32[4,1,4096]{2,1,0:T(1,128)} %reshape.259), calls=%async_computation | async-start | bytes 131072 | tf_op jit(solution)/shard_map/all_to_all | solution.py:41
  16.0 0.7 convert_element_type.101
  16.7 0.7 broadcast_compare_fusion
  17.3 0.6 dynamic_slice.19
  17.9 0.7 dynamic_slice.18
  18.6 0.7 dynamic_slice.16
  19.3 0.9 convert_reduce_fusion.1
  20.2 0.9 fusion.50
  21.1 0.7 compare_convert_fusion
  21.9 1.9 fusion.92
  23.7 0.7 convert_element_type.87
  24.5 31.5 %all-gather.1 = bf16[128,1,256]{2,0,1:T(8,128)(2,1)S(1)} all-gather(bf16[16,1,256]{2,0,1:T(8,128)(2,1)S(1)} %get-tuple-element.7), channel_id=3, replica_groups=mesh['row'=8,'col'=4] {'row'}, dimensions={0}, use_global_device_ids=true | all-gather | bytes 73728 | tf_op jit(solution)/shard_map/all_gather | solution.py:52
  56.1 30.5 %all-gather = bf16[128,1,256]{2,0,1:T(8,128)(2,1)S(1)} all-gather(bf16[16,1,256]{2,0,1:T(8,128)(2,1)S(1)} %get-tuple-element.8), channel_id=2, replica_groups=mesh['row'=8,'col'=4] {'row'}, dimensions={0}, use_global_device_ids=true | all-gather | bytes 73728 | tf_op jit(solution)/shard_map/all_gather | solution.py:53
  86.6 0.7 copy.89
  87.4 0.5 broadcast.233
  88.0 0.8 reduce
  89.2 0.9 fusion.10
  90.4 1.1 convolution_bitcast_fusion.2
  91.6 1.5 fusion.74
  93.3 0.7 broadcast_multiply_fusion
  94.0 0.8 copy.95
  94.8 31.4 %all-reduce.2.cloned.1.call-done = f32[16,1024]{1,0:T(8,128)} async-done(((f32[16,1024]{1,0:T(8,128)}), f32[16,1024]{1,0:T(8,128)}) %all-reduce.2.cloned.1.call-update) | async-done | bytes 65552 | tf_op jit(solution)/shard_map/psum | solution.py:80
  126.2 1.0 convert_reduce_fusion.2
  127.4 0.2 convolution_convert_fusion
  127.7 30.7 %all_gather.14 = bf16[128,64]{1,0:T(8,128)(2,1)S(1)} all-gather(bf16[16,64]{1,0:T(8,128)(2,1)S(1)} %get-tuple-element.12), channel_id=1, replica_groups=mesh['row'=8,'col'=4] {'row'}, dimensions={0}, use_global_device_ids=true | all-gather | bytes 18432 | tf_op jit(solution)/shard_map/all_gather | solution.py:87
  158.4 1.1 fusion.94
  159.6 0.3 multiply_reduce_fusion.2
  159.8 0.4 copy-done.2
  160.3 1.3 fusion.32
  161.6 0.8 fusion.18
  162.5 1.2 copy.101
  163.7 39.1 %all-gather.4.cloned.1.call-done = bf16[128,32,128]{2,1,0:T(8,128)(2,1)} async-done(((bf16[16,32,128]{2,1,0:T(8,128)(2,1)}), bf16[128,32,128]{2,1,0:T(8,128)(2,1)}) %all-gather.4.cloned.1.call-update) | async-done | bytes 1048592 | tf_op jit(solution)/shard_map/all_gather | solution.py:113
  202.8 7.3 %copy.102 = bf16[128,32,128]{1,0,2:T(8,128)(2,1)} copy(bf16[128,32,128]{2,1,0:T(8,128)(2,1)} %all-gather.4.cloned.1.call-done) | data formatting | bytes 2097152 | tf_op jit(solution)/shard_map/all_gather | solution.py:113
  210.0 5.6 %convolution_bitcast_fusion = f32[128,16,128]{0,1,2:T(8,128)} fusion(bf16[16,32,128]{1,0,2:T(8,128)(2,1)} %copy.101, bf16[128,32,128]{1,0,2:T(8,128)(2,1)} %copy.102), kind=kOutput, calls=%fused_computation.4 | convolution fusion | flops 16777216 | bytes 2228224 | tf_op jit(solution)/shard_map/jkc,ikc->jic/dot_general | solution.py:115
  215.6 2.8 %copy.103 = f32[128,16,128]{2,1,0:T(8,128)} copy(f32[128,16,128]{0,1,2:T(8,128)} %convolution_bitcast_fusion) | data formatting | bytes 2097152 | tf_op jit(solution)/shard_map/jkc,ikc->jic/transpose | solution.py:115
  218.4 23.7 %reduce-scatter.2.cloned.1.call-done = f32[32,16,128]{2,1,0:T(8,128)} async-done(((f32[128,16,128]{2,1,0:T(8,128)}), f32[32,16,128]{2,1,0:T(8,128)}) %reduce-scatter.2.cloned.1.call-update) | async-done | bytes 262160 | tf_op jit(solution)/shard_map/reduce_scatter | solution.py:114
  242.1 1.1 bitcast_reduce_fusion
  243.4 1.2 multiply_reduce_fusion.1
  244.7 1.2 multiply_convert_fusion.1
  245.9 1.3 fusion.95
  247.2 0.3 multiply_reduce_fusion
  247.5 0.4 copy-done.1
  248.1 1.3 fusion.4
  249.4 1.6 add_convert_fusion
  (60 shorter events, 2.3 us)
Async XLA Ops:
  7.2 14.7 %copy-start = (bf16[1024,4,256]{2,1,0:T(4,128)(2,1)S(1)}, bf16[1024,4,256]{2,1,0:T(4,128)(2,1)}, u32[]{:S(2)}) copy-start(bf16[1024,4,256]{2,1,0:T(4,128)(2,1)} %param.18) | copy-start | bytes 6291460
  9.6 77.8 %copy-start.10 = (f32[32]{0:T(128)S(1)}, f32[32]{0:T(128)}, u32[]{:S(2)}) copy-start(f32[32]{0:T(128)} %param.21) | copy-start | bytes 388
  11.8 75.7 %all-to-all-start = ((f32[4,1,4096]{2,1,0:T(1,128)}), f32[4,1,4096]{2,1,0:T(1,128)S(1)}, u32[]{:S(2)}, u32[]{:S(2)}) async-start(f32[4,1,4096]{2,1,0:T(1,128)} %reshape.259), calls=%async_computation | async-start | bytes 131072 | tf_op jit(solution)/shard_map/all_to_all | solution.py:41
  16.0 110.2 %all-reduce.2.cloned.1.call-start = ((), (), s32[]{:S(2)}) async-start(), calls=%async_computation.2 | async-start | bytes 131072 | tf_op jit(solution)/shard_map/psum | solution.py:80
  21.9 69.8 %copy-start.5 = (bf16[256,1024]{1,0:T(8,128)(2,1)S(1)}, bf16[256,1024]{1,0:T(8,128)(2,1)}, u32[]{:S(2)}) copy-start(bf16[256,1024]{1,0:T(8,128)(2,1)} %param.19) | copy-start | bytes 1572868
  23.7 70.3 %copy-start.6 = (bf16[128,5,128]{2,0,1:T(8,128)(2,1)S(1)}, bf16[128,5,128]{2,0,1:T(8,128)(2,1)}, u32[]{:S(2)}) copy-start(bf16[128,5,128]{2,0,1:T(8,128)(2,1)} %param.24) | copy-start | bytes 491524
  23.7 102.5 %copy-start.4 = (bf16[16,1024]{1,0:T(8,128)(2,1)S(1)}, bf16[16,1024]{1,0:T(8,128)(2,1)}, u32[]{:S(2)}) copy-start(bf16[16,1024]{1,0:T(8,128)(2,1)} %param.14) | copy-start | bytes 98308
  87.4 71.1 %copy-start.3 = (bf16[16,32,128]{2,1,0:T(8,128)(2,1)S(1)}, bf16[16,32,128]{2,1,0:T(8,128)(2,1)}, u32[]{:S(2)}) copy-start(bf16[16,32,128]{2,1,0:T(8,128)(2,1)} %param.15) | copy-start | bytes 393220
  89.2 38.2 %copy-start.8 = (bf16[1024,128]{1,0:T(8,128)(2,1)S(1)}, bf16[1024,128]{1,0:T(8,128)(2,1)}, u32[]{:S(2)}) copy-start(bf16[1024,128]{1,0:T(8,128)(2,1)} %param.22) | copy-start | bytes 786436
  93.2 109.6 %all-gather.4.cloned.1.call-start = ((), (), s32[]{:S(2)}) async-start(), calls=%async_computation.3 | async-start | bytes 1179648 | tf_op jit(solution)/shard_map/all_gather | solution.py:113
  127.2 32.6 %copy-start.7 = (bf16[16,1024]{1,0:T(8,128)(2,1)}, bf16[16,1024]{1,0:T(8,128)(2,1)S(1)}, u32[]{:S(2)}) copy-start(bf16[16,1024]{1,0:T(8,128)(2,1)S(1)} %get-tuple-element.3) | copy-start | bytes 98308
  159.5 0.7 copy-start.2
  162.4 79.7 %reduce-scatter.2.cloned.1.call-start = ((), (), s32[]{:S(2)}) async-start(), calls=%async_computation.4 | async-start | bytes 1310720 | tf_op jit(solution)/shard_map/reduce_scatter | solution.py:114
  245.9 2.2 copy-start.9
  247.2 0.7 copy-start.1
Sparse Core Ops, SparseCore 0:
  93.3 32.8 all-reduce.1
  162.5 40.1 all-gather.3
  218.6 23.5 reduce-scatter.1
where the time goes:
time: 259 us; the launch traced here: 258 us
  waiting for transfers between devices  94.3 us (36%)
  blocking collectives  92.7 us (36%)
  local copies, waits for them, and re-layouts  18.8 us (7%)
  matrix products  17.5 us (7%)
  other arithmetic  16 us (6%)
  between operations  14 us (5%)
  starting transfers between devices  4.32 us (2%)
    all_gather x1, waiting for transfers between devices, per_device(): column_all = lax.all_gather(right_op, 'row', axis=0, tiled=True)  39.1 us
    all_gather x1, blocking collectives, per_device(): lax.all_gather(key_rows, 'row', axis=0, tiled=True)  31.5 us
    psum x1, waiting for transfers between devices, per_device(): update = lax.psum(head_terms, 'col')  31.4 us
    all_gather x1, blocking collectives, per_device(): lax.all_gather(outer_rows[:, half_width:], 'row', axis=0, tiled=True)  30.7 us
    all_gather x1, blocking collectives, per_device(): lax.all_gather(value_rows, 'row', axis=0, tiled=True)  30.5 us
    reduce_scatter x1, waiting for transfers between devices, per_device(): lax.psum_scatter(jnp.einsum('jkc,ikc->jic', column_all, left_op, preferre...  23.7 us
    all_gather x1, local copies, waits for them, and re-layouts, per_device(): column_all = lax.all_gather(right_op, 'row', axis=0, tiled=True)  7.25 us
    dot_general x1, matrix products, per_device(): jnp.einsum('jkc,ikc->jic', column_all, left_op, preferred_element_type=jn...  5.6 us
  transfers between devices with their start and end apart: 4, of which 3 were waited for; matrix products, arithmetic and copies ran while one was open for 5% of the time, Pallas kernels for 0%

commit v1 on v0

--- a/solution.py
+++ b/solution.py
@@ -77,7 +77,10 @@
     ).reshape(rows_here, -1)
     mixed = (gate * gathered).astype(jnp.bfloat16)
     head_terms = jnp.dot(mixed, attention_out, preferred_element_type=jnp.float32)
-    update = lax.psum(head_terms, "col")
+    size, update = (lax.axis_size("col"), head_terms)
+    for hop in [1 << k for k in range(size.bit_length() - 1)]:
+        pairs = [(i, i ^ hop) for i in range(size)]
+        update = update + lax.ppermute(update, "col", pairs)
     sequence_out = (sequence.astype(jnp.float32) + update).astype(jnp.bfloat16)
     normed_out = layer_norm(sequence_out.astype(jnp.float32)).astype(jnp.bfloat16)
     outer_rows = jnp.dot(normed_out, outer_in, preferred_element_type=jnp.float32).astype(

time: 259 us -> 229 us (0.88)
  waiting for transfers between devices: 94.3 us -> 66.1 us
    psum x1 -> x0, waiting for transfers between devices: 31.4 us -> none  [per_device(): update = lax.psum(head_terms, 'col')]
  transfers between devices with their start and end apart: 4 -> 5, of which waited for: 3 -> 4; matrix products, arithmetic and copies ran while one was open for 5% -> 5% of each run, Pallas kernels for 0% -> 0%
where the time goes in v1:
time: 229 us; the launch traced here: 228 us
  blocking collectives  92.6 us (40%)
  waiting for transfers between devices  66.1 us (29%)
  local copies, waits for them, and re-layouts  17.7 us (8%)
  matrix products  16.9 us (7%)
  other arithmetic  14.5 us (6%)
  between operations  14.3 us (6%)
  starting transfers between devices  6.27 us (3%)
    all_gather x1, waiting for transfers between devices, per_device(): column_all = lax.all_gather(right_op, 'row', axis=0, tiled=True)  40.4 us
    all_gather x1, blocking collectives, per_device(): lax.all_gather(key_rows, 'row', axis=0, tiled=True)  31.5 us
    all_gather x1, blocking collectives, per_device(): lax.all_gather(outer_rows[:, half_width:], 'row', axis=0, tiled=True)  30.6 us
    all_gather x1, blocking collectives, per_device(): lax.all_gather(value_rows, 'row', axis=0, tiled=True)  30.5 us
    reduce_scatter x1, waiting for transfers between devices, per_device(): lax.psum_scatter(jnp.einsum('jkc,ikc->jic', column_all, left_op, preferre...  23.7 us
    all_gather x1, local copies, waits for them, and re-layouts, per_device(): column_all = lax.all_gather(right_op, 'row', axis=0, tiled=True)  7.25 us
    dot_general x1, matrix products, per_device(): jnp.einsum('jkc,ikc->jic', column_all, left_op, preferred_element_type=jn...  5.6 us
  transfers between devices with their start and end apart: 5, of which 4 were waited for; matrix products, arithmetic and copies ran while one was open for 5% of the time, Pallas kernels for 0%

profile of v1, /device:TPU:0, one launch (start us, length us, event | category | flops | bytes accessed | tf_op | source)
XLA Modules:
  0.0 228.5 jit_solution(8431120564355698262)
XLA Ops:
  7.2 1.2 convert_reduce_fusion
  8.4 1.2 fusion.14
  9.6 1.2 convolution_bitcast_fusion.1
  11.0 0.8 reshape.259
  11.8 4.2 %all-to-all-start = ((f32[4,1,4096]{2,1,0:T(1,128)}), f32[4,1,4096]{2,1,0:T(1,128)S(1)}, u32[]{:S(2)}, u32[]{:S(2)}) async-start(f32[4,1,4096]{2,1,0:T(1,128)} %reshape.259), calls=%async_computation | async-start | bytes 131072 | tf_op jit(solution)/shard_map/all_to_all | solution.py:41
  16.0 0.7 broadcast_compare_fusion
  16.7 0.9 convert_reduce_fusion.1
  17.6 0.9 fusion.50
  18.5 0.7 dynamic_slice.16
  19.3 0.7 compare_convert_fusion
  20.0 1.9 fusion.92
  21.9 0.7 convert_element_type.87
  22.6 31.5 %all-gather.1 = bf16[128,1,256]{2,0,1:T(8,128)(2,1)S(1)} all-gather(bf16[16,1,256]{2,0,1:T(8,128)(2,1)S(1)} %get-tuple-element.7), channel_id=3, replica_groups=mesh['row'=8,'col'=4] {'row'}, dimensions={0}, use_global_device_ids=true | all-gather | bytes 73728 | tf_op jit(solution)/shard_map/all_gather | solution.py:52
  54.2 30.5 %all-gather = bf16[128,1,256]{2,0,1:T(8,128)(2,1)S(1)} all-gather(bf16[16,1,256]{2,0,1:T(8,128)(2,1)S(1)} %get-tuple-element.8), channel_id=2, replica_groups=mesh['row'=8,'col'=4] {'row'}, dimensions={0}, use_global_device_ids=true | all-gather | bytes 73728 | tf_op jit(solution)/shard_map/all_gather | solution.py:53
  84.8 0.7 copy.89
  85.6 0.5 broadcast.233
  86.1 0.8 reduce
  87.4 0.9 fusion.10
  88.5 1.1 convolution_bitcast_fusion.2
  89.8 0.9 fusion.74
  90.7 0.7 convert_element_type.101
  91.5 0.4 collective-permute-done
  92.0 2.0 collective-permute-start.1
  94.0 0.8 copy.95
  94.8 1.5 collective-permute-done.1
  96.5 0.2 fusion.52
  96.7 0.2 convolution_convert_fusion
  97.0 30.6 %all_gather.14 = bf16[128,64]{1,0:T(8,128)(2,1)S(1)} all-gather(bf16[16,64]{1,0:T(8,128)(2,1)S(1)} %get-tuple-element.12), channel_id=1, replica_groups=mesh['row'=8,'col'=4] {'row'}, dimensions={0}, use_global_device_ids=true | all-gather | bytes 18432 | tf_op jit(solution)/shard_map/all_gather | solution.py:90
  127.7 1.1 fusion.94
  128.8 0.3 multiply_reduce_fusion.2
  129.1 0.4 copy-done.2
  129.5 1.3 fusion.32
  130.8 0.8 fusion.18
  131.7 1.2 copy.101
  132.9 40.4 %all-gather.4.cloned.1.call-done = bf16[128,32,128]{2,1,0:T(8,128)(2,1)} async-done(((bf16[16,32,128]{2,1,0:T(8,128)(2,1)}), bf16[128,32,128]{2,1,0:T(8,128)(2,1)}) %all-gather.4.cloned.1.call-update) | async-done | bytes 1048592 | tf_op jit(solution)/shard_map/all_gather | solution.py:116
  173.3 7.3 %copy.102 = bf16[128,32,128]{1,0,2:T(8,128)(2,1)} copy(bf16[128,32,128]{2,1,0:T(8,128)(2,1)} %all-gather.4.cloned.1.call-done) | data formatting | bytes 2097152 | tf_op jit(solution)/shard_map/all_gather | solution.py:116
  180.6 5.6 %convolution_bitcast_fusion = f32[128,16,128]{0,1,2:T(8,128)} fusion(bf16[16,32,128]{1,0,2:T(8,128)(2,1)} %copy.101, bf16[128,32,128]{1,0,2:T(8,128)(2,1)} %copy.102), kind=kOutput, calls=%fused_computation.4 | convolution fusion | flops 16777216 | bytes 2228224 | tf_op jit(solution)/shard_map/jkc,ikc->jic/dot_general | solution.py:118
  186.2 2.8 %copy.103 = f32[128,16,128]{2,1,0:T(8,128)} copy(f32[128,16,128]{0,1,2:T(8,128)} %convolution_bitcast_fusion) | data formatting | bytes 2097152 | tf_op jit(solution)/shard_map/jkc,ikc->jic/transpose | solution.py:118
  189.0 23.7 %reduce-scatter.2.cloned.1.call-done = f32[32,16,128]{2,1,0:T(8,128)} async-done(((f32[128,16,128]{2,1,0:T(8,128)}), f32[32,16,128]{2,1,0:T(8,128)}) %reduce-scatter.2.cloned.1.call-update) | async-done | bytes 262160 | tf_op jit(solution)/shard_map/reduce_scatter | solution.py:117
  212.7 1.1 bitcast_reduce_fusion
  213.9 1.2 multiply_reduce_fusion.1
  215.3 1.2 multiply_convert_fusion.1
  216.5 1.3 fusion.95
  217.8 0.3 multiply_reduce_fusion
  218.1 0.4 copy-done.1
  218.4 0.2 multiply_convert_fusion
  218.7 1.3 fusion.4
  220.0 1.6 add_convert_fusion
  (62 shorter events, 2.2 us)
Async XLA Ops:
  7.2 12.8 %copy-start = (bf16[1024,4,256]{2,1,0:T(4,128)(2,1)S(1)}, bf16[1024,4,256]{2,1,0:T(4,128)(2,1)}, u32[]{:S(2)}) copy-start(bf16[1024,4,256]{2,1,0:T(4,128)(2,1)} %param.18) | copy-start | bytes 6291460
  9.6 75.9 %copy-start.10 = (f32[32]{0:T(128)S(1)}, f32[32]{0:T(128)}, u32[]{:S(2)}) copy-start(f32[32]{0:T(128)} %param.21) | copy-start | bytes 388
  11.8 73.8 %all-to-all-start = ((f32[4,1,4096]{2,1,0:T(1,128)}), f32[4,1,4096]{2,1,0:T(1,128)S(1)}, u32[]{:S(2)}, u32[]{:S(2)}) async-start(f32[4,1,4096]{2,1,0:T(1,128)} %reshape.259), calls=%async_computation | async-start | bytes 131072 | tf_op jit(solution)/shard_map/all_to_all | solution.py:41
  16.0 157.3 %all-gather.4.cloned.1.call-start = ((), (), s32[]{:S(2)}) async-start(), calls=%async_computation.2 | async-start | bytes 1179648 | tf_op jit(solution)/shard_map/all_gather | solution.py:116
  20.0 69.8 %copy-start.5 = (bf16[256,1024]{1,0:T(8,128)(2,1)S(1)}, bf16[256,1024]{1,0:T(8,128)(2,1)}, u32[]{:S(2)}) copy-start(bf16[256,1024]{1,0:T(8,128)(2,1)} %param.19) | copy-start | bytes 1572868
  21.9 72.2 %copy-start.6 = (bf16[128,5,128]{2,0,1:T(8,128)(2,1)S(1)}, bf16[128,5,128]{2,0,1:T(8,128)(2,1)}, u32[]{:S(2)}) copy-start(bf16[128,5,128]{2,0,1:T(8,128)(2,1)} %param.24) | copy-start | bytes 491524
  21.9 74.5 %copy-start.4 = (bf16[16,1024]{1,0:T(8,128)(2,1)S(1)}, bf16[16,1024]{1,0:T(8,128)(2,1)}, u32[]{:S(2)}) copy-start(bf16[16,1024]{1,0:T(8,128)(2,1)} %param.14) | copy-start | bytes 98308
  86.9 40.8 %copy-start.3 = (bf16[16,32,128]{2,1,0:T(8,128)(2,1)S(1)}, bf16[16,32,128]{2,1,0:T(8,128)(2,1)}, u32[]{:S(2)}) copy-start(bf16[16,32,128]{2,1,0:T(8,128)(2,1)} %param.15) | copy-start | bytes 393220
  87.4 9.3 %copy-start.8 = (bf16[1024,128]{1,0:T(8,128)(2,1)S(1)}, bf16[1024,128]{1,0:T(8,128)(2,1)}, u32[]{:S(2)}) copy-start(bf16[1024,128]{1,0:T(8,128)(2,1)} %param.22) | copy-start | bytes 786436
  90.7 1.3 collective-permute-start
  92.0 4.4 %collective-permute-start.1 = (f32[16,1024]{1,0:T(8,128)S(1)}, f32[16,1024]{1,0:T(8,128)S(1)}, u32[]{:S(2)}, u32[]{:S(2)}) collective-permute-start(f32[16,1024]{1,0:T(8,128)S(1)} %add.120), channel_id=1, source_target_pairs={{0,2},{1,3},{2,0},{3,1},{4,6},{5,7},{6,4},{7,5},{8,10},{9,11},{10,... | collective-permute-start | bytes 196616 | tf_op jit(solution)/shard_map/ppermute | solution.py:83
  96.5 32.6 %copy-start.7 = (bf16[16,1024]{1,0:T(8,128)(2,1)}, bf16[16,1024]{1,0:T(8,128)(2,1)S(1)}, u32[]{:S(2)}) copy-start(bf16[16,1024]{1,0:T(8,128)(2,1)S(1)} %get-tuple-element.3) | copy-start | bytes 98308
  128.8 0.7 copy-start.2
  131.6 81.0 %reduce-scatter.2.cloned.1.call-start = ((), (), s32[]{:S(2)}) async-start(), calls=%async_computation.3 | async-start | bytes 1310720 | tf_op jit(solution)/shard_map/reduce_scatter | solution.py:117
  216.4 2.2 copy-start.9
  217.8 0.7 copy-start.1
Sparse Core Ops, SparseCore 0:
  131.8 41.5 all-gather.3
  189.1 23.5 reduce-scatter.1
